TPU v7x, 32 devices: a whole 2x2x4 slice. The times are simulated.
32 devices in a mesh: doc: 8 (over y, x, core), seq: 4 (over z).
Axes of the slice: x: 2, y: 2, z: 4, core: 2. Of those that a mesh axis runs over, the one named last changes fastest.
Arguments:
- inputs: bfloat16 [16, 1024, 768], P('doc', 'seq'), may hold values from -6 to 6
- attn_gain: float32 [768], replicated, may hold values from 0.5 to 1.5
- qkv_weight: bfloat16 [768, 2304], replicated, may hold values from -0.25 to 0.25
- attn_out_weight: bfloat16 [768, 768], replicated, may hold values from -2 to 2
- mlp_gain: float32 [768], replicated, may hold values from 0.5 to 1.5
- mlp_in_weight: bfloat16 [768, 2304], replicated, may hold values from -0.21875 to 0.21875
- mlp_out_weight: bfloat16 [1152, 768], replicated, may hold values from -0.1875 to 0.1875
- cotangent: bfloat16 [16, 1024, 768], P('doc', 'seq'), may hold values from -6 to 6
Outputs:
- output: bfloat16 [16, 1024, 768], P('doc', 'seq')
- input_grad: bfloat16 [16, 1024, 768], P('doc', 'seq')
- attn_gain_grad: float32 [768], replicated
- qkv_weight_grad: float32 [768, 2304], replicated
- attn_out_weight_grad: float32 [768, 768], replicated
- mlp_gain_grad: float32 [768], replicated
- mlp_in_weight_grad: float32 [768, 2304], replicated
- mlp_out_weight_grad: float32 [1152, 768], replicated
All inputs are finite; a program needn't handle non-finite values.
Results may differ from a plain program's by a relative error of at most 0.015.
Values may be sent and summed in bfloat16 or wider, within the bound.
A program may use at most 128 MiB of HBM per device.

v0:
```python
import jax
import jax.numpy as jnp
from jax import lax
from jax.sharding import PartitionSpec as P

HEAD_DIM = 64
ROPE_THETA = 160000.0
NORM_EPSILON = 1e-05


def norm_rows(values, scale_gain):
    row_mean = jnp.mean(values, axis=-1, keepdims=True)
    centered = values - row_mean
    variance = jnp.mean(centered * centered, axis=-1, keepdims=True)
    return centered * lax.rsqrt(variance + NORM_EPSILON) * scale_gain


def rotary_tables(positions, head_width):
    half_width = head_width // 2
    frequency = ROPE_THETA ** (-(jnp.arange(half_width, dtype=jnp.float32) * 2.0) / head_width)
    angles = positions.astype(jnp.float32)[:, None] * frequency[None, :]
    angles = jnp.concatenate([angles, angles], axis=-1)
    return (jnp.cos(angles)[:, None, :], jnp.sin(angles)[:, None, :])


def rotate(values, cosine_table, sine_table):
    half_width = values.shape[-1] // 2
    turned = jnp.concatenate([-values[..., half_width:], values[..., :half_width]], axis=-1)
    return values * cosine_table + turned * sine_table


def rotate_back(gradient, cosine_table, sine_table):
    half_width = gradient.shape[-1] // 2
    sined = gradient * sine_table
    turned = jnp.concatenate([sined[..., half_width:], -sined[..., :half_width]], axis=-1)
    return gradient * cosine_table + turned


def gelu_product(gate_up):
    half_width = gate_up.shape[-1] // 2
    return jax.nn.gelu(gate_up[..., :half_width], approximate=False) * gate_up[..., half_width:]


def split_heads(columns):
    return columns.reshape(columns.shape[0], columns.shape[1] // HEAD_DIM, HEAD_DIM)


def attend_forward(queries, key_rows, value_rows):
    length, features = queries.shape
    scores = (
        jnp.einsum(
            "qhd,khd->hqk",
            split_heads(queries),
            split_heads(key_rows),
            preferred_element_type=jnp.float32,
        )
        * 0.125
    )
    row_max = jnp.max(scores, axis=-1, keepdims=True)
    exp_scores = jnp.exp(scores - row_max)
    row_total = jnp.sum(exp_scores, axis=-1, keepdims=True)
    softmax_low = (exp_scores / row_total).astype(jnp.bfloat16)
    mixed_rows = jnp.einsum(
        "hqk,khd->qhd", softmax_low, split_heads(value_rows), preferred_element_type=jnp.float32
    )
    return (
        mixed_rows.reshape(length, features).astype(jnp.bfloat16),
        (row_max + jnp.log(row_total))[..., 0],
    )


def attend_backward(queries, key_rows, value_rows, grad_mixed, log_total, cosine_table, sine_table):
    length, features = queries.shape
    query_heads = split_heads(queries)
    key_heads = split_heads(key_rows)
    value_heads = split_heads(value_rows)
    grad_heads = split_heads(grad_mixed)
    scores = (
        jnp.einsum("qhd,khd->hqk", query_heads, key_heads, preferred_element_type=jnp.float32)
        * 0.125
    )
    softmax_out = jnp.exp(scores - log_total[..., None])
    grad_soft = jnp.einsum(
        "qhd,khd->hqk", grad_heads, value_heads, preferred_element_type=jnp.float32
    )
    row_inner = jnp.sum(softmax_out * grad_soft, axis=-1, keepdims=True)
    grad_scores = (softmax_out * (grad_soft - row_inner)).astype(jnp.bfloat16)
    grad_query = (
        jnp.einsum("hqk,khd->qhd", grad_scores, key_heads, preferred_element_type=jnp.float32)
        * 0.125
    )
    grad_key = (
        jnp.einsum("hqk,qhd->khd", grad_scores, query_heads, preferred_element_type=jnp.float32)
        * 0.125
    )
    grad_value = jnp.einsum(
        "hqk,qhd->khd",
        softmax_out.astype(jnp.bfloat16),
        grad_heads,
        preferred_element_type=jnp.float32,
    )
    grad_query = (
        rotate_back(grad_query, cosine_table, sine_table)
        .reshape(length, features)
        .astype(jnp.bfloat16)
    )
    grad_key = (
        rotate_back(grad_key, cosine_table, sine_table)
        .reshape(length, features)
        .astype(jnp.bfloat16)
    )
    return (grad_query, grad_key, grad_value.reshape(length, features).astype(jnp.bfloat16))


def per_device(
    inputs,
    attn_gain,
    qkv_weight,
    attn_out_weight,
    mlp_gain,
    mlp_in_weight,
    mlp_out_weight,
    cotangent,
):
    doc_count, row_count, features = inputs.shape
    token_count = doc_count * row_count
    length = row_count * lax.axis_size("seq")
    flat_in = inputs.reshape(token_count, features).astype(jnp.float32)
    normed = norm_rows(flat_in, attn_gain).astype(jnp.bfloat16)
    projected = jnp.dot(normed, qkv_weight, preferred_element_type=jnp.float32)
    projected = projected.reshape(doc_count, row_count, 3 * features)
    local_cos, local_sin = rotary_tables(
        lax.axis_index("seq") * row_count + jnp.arange(row_count, dtype=jnp.int32), HEAD_DIM
    )

    def turned_low(columns):
        shaped = columns.reshape(doc_count, row_count, features // HEAD_DIM, HEAD_DIM)
        return (
            rotate(shaped, local_cos, local_sin)
            .reshape(doc_count, row_count, features)
            .astype(jnp.bfloat16)
        )

    queries = turned_low(projected[..., :features])
    key_rows = turned_low(projected[..., features : 2 * features])
    value_rows = projected[..., 2 * features :].astype(jnp.bfloat16)
    head_queries, head_keys, head_values = (
        lax.all_to_all(queries, "seq", split_axis=2, concat_axis=1, tiled=True),
        lax.all_to_all(key_rows, "seq", split_axis=2, concat_axis=1, tiled=True),
        lax.all_to_all(value_rows, "seq", split_axis=2, concat_axis=1, tiled=True),
    )
    mixed_heads, log_total = lax.map(
        lambda bundle: attend_forward(*bundle), (head_queries, head_keys, head_values)
    )
    attended = lax.all_to_all(mixed_heads, "seq", split_axis=1, concat_axis=2, tiled=True).reshape(
        token_count, features
    )
    hidden_res = flat_in + jnp.dot(attended, attn_out_weight, preferred_element_type=jnp.float32)
    normed_two = norm_rows(hidden_res, mlp_gain).astype(jnp.bfloat16)
    gate_up = jnp.dot(normed_two, mlp_in_weight, preferred_element_type=jnp.float32)
    inner_act, inner_pull = jax.vjp(gelu_product, gate_up)
    inner_act = inner_act.astype(jnp.bfloat16)
    result = hidden_res + jnp.dot(inner_act, mlp_out_weight, preferred_element_type=jnp.float32)
    output = result.astype(jnp.bfloat16).reshape(doc_count, row_count, features)
    upstream = cotangent.reshape(token_count, features)
    grad_mlp_out = jnp.einsum("tf,td->fd", inner_act, upstream, preferred_element_type=jnp.float32)
    grad_inner = jnp.einsum(
        "td,fd->tf", upstream, mlp_out_weight, preferred_element_type=jnp.float32
    )
    grad_gate_up = inner_pull(grad_inner)[0].astype(jnp.bfloat16)
    grad_mlp_in = jnp.einsum(
        "td,tf->df", normed_two, grad_gate_up, preferred_element_type=jnp.float32
    )
    grad_normed_two = jnp.einsum(
        "tf,df->td", grad_gate_up, mlp_in_weight, preferred_element_type=jnp.float32
    )
    _, second_pull = jax.vjp(norm_rows, hidden_res, mlp_gain)
    grad_hidden, grad_mlp_gain = second_pull(grad_normed_two)
    grad_hidden = grad_hidden + upstream.astype(jnp.float32)
    grad_branch = grad_hidden.astype(jnp.bfloat16)
    grad_attn_out = jnp.einsum(
        "td,te->de", attended, grad_branch, preferred_element_type=jnp.float32
    )
    grad_attended = jnp.einsum(
        "te,de->td", grad_branch, attn_out_weight, preferred_element_type=jnp.float32
    )
    grad_attended = grad_attended.astype(jnp.bfloat16).reshape(doc_count, row_count, features)
    grad_mixed = lax.all_to_all(grad_attended, "seq", split_axis=2, concat_axis=1, tiled=True)
    full_cos, full_sin = rotary_tables(jnp.arange(length, dtype=jnp.int32), HEAD_DIM)
    grad_head_q, grad_head_k, grad_head_v = lax.map(
        lambda bundle: attend_backward(*bundle, full_cos, full_sin),
        (head_queries, head_keys, head_values, grad_mixed, log_total),
    )
    grad_tok_q, grad_tok_k, grad_tok_v = (
        lax.all_to_all(grad_head_q, "seq", split_axis=1, concat_axis=2, tiled=True),
        lax.all_to_all(grad_head_k, "seq", split_axis=1, concat_axis=2, tiled=True),
        lax.all_to_all(grad_head_v, "seq", split_axis=1, concat_axis=2, tiled=True),
    )
    grad_tok_q = grad_tok_q.reshape(token_count, features)
    grad_tok_k = grad_tok_k.reshape(token_count, features)
    grad_tok_v = grad_tok_v.reshape(token_count, features)
    grad_qkv = jnp.concatenate(
        [
            jnp.einsum("td,te->de", normed, grad_tok_q, preferred_element_type=jnp.float32),
            jnp.einsum("td,te->de", normed, grad_tok_k, preferred_element_type=jnp.float32),
            jnp.einsum("td,te->de", normed, grad_tok_v, preferred_element_type=jnp.float32),
        ],
        axis=1,
    )
    grad_normed = jnp.einsum(
        "te,de->td", grad_tok_q, qkv_weight[:, :features], preferred_element_type=jnp.float32
    )
    grad_normed = grad_normed + jnp.einsum(
        "te,de->td",
        grad_tok_k,
        qkv_weight[:, features : 2 * features],
        preferred_element_type=jnp.float32,
    )
    grad_normed = grad_normed + jnp.einsum(
        "te,de->td", grad_tok_v, qkv_weight[:, 2 * features :], preferred_element_type=jnp.float32
    )
    _, first_pull = jax.vjp(norm_rows, flat_in, attn_gain)
    grad_input, grad_attn_gain = first_pull(grad_normed)
    grad_input = (
        (grad_input + grad_hidden).astype(jnp.bfloat16).reshape(doc_count, row_count, features)
    )
    summed = lax.psum(
        (grad_attn_gain, grad_qkv, grad_attn_out, grad_mlp_gain, grad_mlp_in, grad_mlp_out),
        ("doc", "seq"),
    )
    return (output, grad_input, summed[0], summed[1], summed[2], summed[3], summed[4], summed[5])


def solution(mesh):
    placed = (P("doc", "seq", None), P(), P(), P(), P(), P(), P(), P("doc", "seq", None))
    return jax.shard_map(
        per_device,
        mesh=mesh,
        in_specs=placed,
        out_specs=(P("doc", "seq", None), P("doc", "seq", None), P(), P(), P(), P(), P(), P()),
        check_vma=False,
    )
```

profile of v0, /device:TPU:0, one launch (start us, length us, event | category | flops | bytes accessed | tf_op | source)
XLA Modules:
  0.0 743.3 jit_solution(14533819958164597936)
XLA Ops:
  12.8 4.3 fusion.13
  23.3 6.3 all-to-all-start
  29.6 3.9 fusion.58
  59.2 5.0 add_convert_fusion.3
  67.2 5.1 all-to-all-start.1
  75.3 16.6 %all-to-all-done.1 = bf16[2,256,768]{1,0,2:T(2,128)(2,1)} async-done(((bf16[2,256,768]{1,0,2:T(2,128)(2,1)}), bf16[2,256,768]{1,0,2:T(2,128)(2,1)}, u32[]{:S(2)}, u32[]{:S(2)}) %all-to-all-start.1) | async-done | bytes 786464 | tf_op jit(solution)/shard_map/all_to_all | solution.py:148
  91.9 4.4 all-to-all-start.2
  100.8 15.2 %all-to-all-done.2 = bf16[2,256,768]{1,0,2:T(2,128)(2,1)} async-done(((bf16[2,256,768]{1,0,2:T(2,128)(2,1)}), bf16[2,256,768]{1,0,2:T(2,128)(2,1)}, u32[]{:S(2)}, u32[]{:S(2)}) %all-to-all-start.2) | async-done | bytes 786464 | tf_op jit(solution)/shard_map/all_to_all | solution.py:149
  119.2 19.5 %while.26 = (s32[]{:T(128)}, bf16[2,1024,192]{1,2,0:T(8,128)(2,1)}, f32[2,3,1024]{2,1,0:T(4,128)}, bf16[2,1024,192]{1,2,0:T(8,128)(2,1)}, bf16[2,1024,192]{1,2,0...) while((s32[]{:T(128)}, bf16[2,1024,192]{1,2,0:T(8,128)(2,1)}, f32[2,3,1024]{2,1,0:T(4,128)}, ...), condition=%wide.region_5.6_spmd, body=%wide.region_2.5_spmd.sunk | while | flops 833811456 | bytes 48861340 | solution.py:152
  142.3 29.5 %all_to_all.132 = bf16[2,1024,192]{2,0,1:T(2,128)(2,1)} all-to-all(bf16[2,1024,192]{2,0,1:T(2,128)(2,1)} %copy.86), channel_id=1, replica_groups=mesh['doc'=8,'seq'=4] {'seq'}, dimensions={1} | all-to-all | bytes 1572864 | tf_op jit(solution)/shard_map/all_to_all | solution.py:155
  171.8 5.9 copy.87
  184.3 5.6 fusion.39
  205.8 17.4 %all-to-all-done.4 = bf16[2,256,768]{1,0,2:T(2,128)(2,1)S(1)} async-done(((bf16[2,256,768]{1,0,2:T(2,128)(2,1)}), bf16[2,256,768]{1,0,2:T(2,128)(2,1)S(1)}, u32[]{:S(2)}, u32[]{:S(2)}) %all-to-all-start.4) | async-done | bytes 786464 | tf_op jit(solution)/shard_map/all_to_all | solution.py:188
  227.2 60.3 %while.27 = (s32[]{:T(128)}, bf16[2,1024,192]{1,2,0:T(8,128)(2,1)}, bf16[2,1024,192]{1,2,0:T(8,128)(2,1)}, bf16[2,1024,192]{1,2,0:T(8,128)(2,1)}, bf16[2,1024,19...) while((s32[]{:T(128)}, bf16[2,1024,192]{1,2,0:T(8,128)(2,1)}, ...), condition=%wide.region_12.13_spmd, body=%wide.region_10.12_spmd.sunk | while | flops 2053501952 | bytes 154489168 | solution.py:190
  238.6 3.7 multiply_reduce_fusion.8
  242.3 5.3 multiply_convert_fusion.6
  247.6 4.1 convolution_bitcast_fusion.3
  268.8 3.7 multiply_reduce_fusion.8
  272.5 5.3 multiply_convert_fusion.6
  277.8 4.1 convolution_bitcast_fusion.3
  296.8 23.1 %all-to-all-done.7 = bf16[2,1024,192]{2,0,1:T(2,128)(2,1)S(1)} async-done(((bf16[2,1024,192]{2,0,1:T(2,128)(2,1)}), bf16[2,1024,192]{2,0,1:T(2,128)(2,1)S(1)}, u32[]{:S(2)}, u32[]{:S(2)}) %all-to-all-start.7) | async-done | bytes 786464 | tf_op jit(solution)/shard_map/all_to_all | solution.py:197
  325.5 23.1 %all-to-all-done.5 = bf16[2,1024,192]{2,0,1:T(2,128)(2,1)S(1)} async-done(((bf16[2,1024,192]{2,0,1:T(2,128)(2,1)}), bf16[2,1024,192]{2,0,1:T(2,128)(2,1)S(1)}, u32[]{:S(2)}, u32[]{:S(2)}) %all-to-all-start.5) | async-done | bytes 786464 | tf_op jit(solution)/shard_map/all_to_all | solution.py:195
  348.6 4.2 all-to-all-start.6
  360.9 5.2 fusion.40
  366.1 4.7 copy.96
  371.9 5.7 copy.92
  379.8 5.7 copy.94
  394.9 4.0 add_convert_fusion.2
  403.7 43.1 %all-reduce.2 = (f32[768]{0:T(1024)}, f32[768]{0:T(1024)}) all-reduce(f32[768]{0:T(1024)S(1)} %get-tuple-element.139, f32[768]{0:T(1024)S(1)} %copy-done.49), channel_id=1, replica_groups=mesh['doc'=8,'seq'=4] {'doc','seq'}, use_global_device_ids=true, to_apply=%region_16.17 | all-reduce | flops 1536 | bytes 12288 | tf_op jit(solution)/shard_map/psum | solution.py:227
  449.8 268.4 %all-reduce.6.cloned.1.call-done = (f32[768,2304]{0,1:T(8,128)}, f32[768,768]{1,0:T(8,128)}, f32[768,2304]{1,0:T(8,128)}, f32[1152,768]{1,0:T(8,128)}) async-done(((f32[768,2304]{0,1:T(8,128)}, f32[768,768]{1,0:T(8,128)}, f32[768,2304]{1,0:T(8,128)}, f32[1152,768]{1,0:T(8,128)}), (f32[768,2304]{0,1:T(8,128)}, f32[768,768]{1,0:T(8,128)}, f32[768,2304]{1,0:T(8,128)}, ...) | async-done | bytes 20054032 | tf_op jit(solution)/shard_map/psum | solution.py:227
  718.3 8.1 %copy.97 = f32[768,2304]{1,0:T(8,128)} copy(f32[768,2304]{0,1:T(8,128)} %get-tuple-element.177) | data formatting | bytes 14155776
  727.8 6.6 copy.145
  (252 shorter events, 180.5 us)
Async XLA Ops:
  7.2 174.9 %copy-start = (bf16[768,2304]{1,0:T(8,128)(2,1)S(1)}, bf16[768,2304]{1,0:T(8,128)(2,1)}, u32[]{:S(2)}) copy-start(bf16[768,2304]{1,0:T(8,128)(2,1)} %param.17) | copy-start | bytes 10616836
  12.8 4.3 copy-start.8
  23.3 43.9 %all-to-all-start = ((bf16[2,256,768]{1,0,2:T(2,128)(2,1)}), bf16[2,256,768]{1,0,2:T(2,128)(2,1)}, u32[]{:S(2)}, u32[]{:S(2)}) async-start(bf16[2,256,768]{1,0,2:T(2,128)(2,1)} %copy.71), calls=%async_computation | async-start | bytes 1572864 | tf_op jit(solution)/shard_map/all_to_all | solution.py:150
  33.5 8.8 %copy-start.50 = (f32[32]{0:T(128)}, f32[32]{0:T(128)S(1)}, u32[]{:S(2)}) copy-start(f32[32]{0:T(128)S(1)} %multiply_power_fusion) | copy-start | bytes 388
  67.2 24.7 %all-to-all-start.1 = ((bf16[2,256,768]{1,0,2:T(2,128)(2,1)}), bf16[2,256,768]{1,0,2:T(2,128)(2,1)}, u32[]{:S(2)}, u32[]{:S(2)}) async-start(bf16[2,256,768]{1,0,2:T(2,128)(2,1)} %copy.78), calls=%async_computation.1 | async-start | bytes 1572864 | tf_op jit(solution)/shard_map/all_to_all | solution.py:148
  91.9 24.0 %all-to-all-start.2 = ((bf16[2,256,768]{1,0,2:T(2,128)(2,1)}), bf16[2,256,768]{1,0,2:T(2,128)(2,1)}, u32[]{:S(2)}, u32[]{:S(2)}) async-start(bf16[2,256,768]{1,0,2:T(2,128)(2,1)} %copy.83), calls=%async_computation.2 | async-start | bytes 1572864 | tf_op jit(solution)/shard_map/all_to_all | solution.py:149
  181.7 13.2 %copy-start.6 = (f32[512,768]{1,0:T(8,128)}, f32[512,768]{1,0:T(8,128)S(1)}, u32[]{:S(2)}) copy-start(f32[512,768]{1,0:T(8,128)S(1)} %get-tuple-element.225) | copy-start | bytes 4718596
  181.8 13.2 %copy-start.41 = (f32[512]{0:T(512)}, f32[512]{0:T(512)S(1)}, u32[]{:S(2)}) copy-start(f32[512]{0:T(512)S(1)} %broadcast_multiply_fusion.3) | copy-start | bytes 6148
  182.1 12.8 %copy-start.43 = (f32[512]{0:T(512)}, f32[512]{0:T(512)S(1)}, u32[]{:S(2)}) copy-start(f32[512]{0:T(512)S(1)} %fusion.46) | copy-start | bytes 6148
  198.7 5.3 copy-start.51
  200.5 22.6 %all-to-all-start.4 = ((bf16[2,256,768]{1,0,2:T(2,128)(2,1)}), bf16[2,256,768]{1,0,2:T(2,128)(2,1)S(1)}, u32[]{:S(2)}, u32[]{:S(2)}) async-start(bf16[2,256,768]{1,0,2:T(2,128)(2,1)} %copy.88), calls=%async_computation.4 | async-start | bytes 1572864 | tf_op jit(solution)/shard_map/all_to_all | solution.py:188
  247.6 4.6 copy-start.2
  277.8 4.6 copy-start.2
  287.5 7.2 copy-start.22
  291.2 28.7 %all-to-all-start.7 = ((bf16[2,1024,192]{2,0,1:T(2,128)(2,1)}), bf16[2,1024,192]{2,0,1:T(2,128)(2,1)S(1)}, u32[]{:S(2)}, u32[]{:S(2)}) async-start(bf16[2,1024,192]{2,0,1:T(2,128)(2,1)} %copy.95), calls=%async_computation.7 | async-start | bytes 2097152 | tf_op jit(solution)/shard_map/all_to_all | solution.py:197
  294.7 28.7 %copy-start.25 = (bf16[2,1024,192]{1,2,0:T(8,128)(2,1)S(1)}, bf16[2,1024,192]{1,2,0:T(8,128)(2,1)}, u32[]{:S(2)}) copy-start(bf16[2,1024,192]{1,2,0:T(8,128)(2,1)} %get-tuple-element.103) | copy-start | bytes 2359300
  319.9 28.7 %copy-start.17 = (bf16[2,1024,192]{2,0,1:T(2,128)(2,1)}, bf16[2,1024,192]{2,0,1:T(2,128)(2,1)S(1)}, u32[]{:S(2)}) copy-start(bf16[2,1024,192]{2,0,1:T(2,128)(2,1)S(1)} %all-to-all-done.7) | copy-start | bytes 2359300
  319.9 28.7 %all-to-all-start.5 = ((bf16[2,1024,192]{2,0,1:T(2,128)(2,1)}), bf16[2,1024,192]{2,0,1:T(2,128)(2,1)S(1)}, u32[]{:S(2)}, u32[]{:S(2)}) async-start(bf16[2,1024,192]{2,0,1:T(2,128)(2,1)} %copy.91), calls=%async_computation.5 | async-start | bytes 2097152 | tf_op jit(solution)/shard_map/all_to_all | solution.py:195
  348.6 8.1 %copy-start.18 = (bf16[2,1024,192]{2,0,1:T(2,128)(2,1)}, bf16[2,1024,192]{2,0,1:T(2,128)(2,1)S(1)}, u32[]{:S(2)}) copy-start(bf16[2,1024,192]{2,0,1:T(2,128)(2,1)S(1)} %all-to-all-done.5) | copy-start | bytes 2359300
  348.6 31.2 %all-to-all-start.6 = ((bf16[2,1024,192]{2,0,1:T(2,128)(2,1)}), bf16[2,1024,192]{2,0,1:T(2,128)(2,1)}, u32[]{:S(2)}, u32[]{:S(2)}) async-start(bf16[2,1024,192]{2,0,1:T(2,128)(2,1)} %copy.93), calls=%async_computation.6 | async-start | bytes 2097152 | tf_op jit(solution)/shard_map/all_to_all | solution.py:196
  352.9 365.4 %all-reduce.6.cloned.1.call-start = ((), (), s32[]{:S(2)}) async-start(), calls=%async_computation.8 | async-start | bytes 40108032 | tf_op jit(solution)/shard_map/psum | solution.py:227
  356.8 4.1 copy-start.36
  356.8 4.1 copy-start.39
  356.8 4.1 copy-start.42
  356.8 4.1 copy-start.44
  377.6 9.3 %copy-start.9 = (bf16[2,256,768]{2,1,0:T(8,128)(2,1)S(1)}, bf16[2,256,768]{2,1,0:T(8,128)(2,1)}, u32[]{:S(2)}) copy-start(bf16[2,256,768]{2,1,0:T(8,128)(2,1)} %copy-done.8) | copy-start | bytes 2359300
  394.9 4.1 copy-start.30
  394.9 4.1 copy-start.37
  402.9 44.0 %copy-start.46 = (f32[512]{0:T(512)S(1)}, f32[512]{0:T(512)}, u32[]{:S(2)}) copy-start(f32[512]{0:T(512)} %copy-done.45) | copy-start | bytes 6148
  718.3 8.1 %copy-start.34 = (f32[768,768]{1,0:T(8,128)S(1)}, f32[768,768]{1,0:T(8,128)}, u32[]{:S(2)}) copy-start(f32[768,768]{1,0:T(8,128)} %get-tuple-element.433) | copy-start | bytes 7077892
  727.8 6.6 copy-start.19
  727.8 8.4 %copy-start.1 = (bf16[768,2304]{1,0:T(8,128)(2,1)S(1)}, bf16[768,2304]{1,0:T(8,128)(2,1)}, u32[]{:S(2)}) copy-start(bf16[768,2304]{1,0:T(8,128)(2,1)} %param.17) | copy-start | bytes 10616836
  (38 other events, 68.1 us)
Sparse Core Ops, SparseCore 0:
  394.3 323.9 all-reduce.5
where the time goes:
time: 752 us; the launch traced here: 743 us
  waiting for transfers between devices  364 us (48%)
  local copies, waits for them, and re-layouts  133 us (18%)
  matrix products  77.8 us (10%)
  blocking collectives  72.7 us (10%)
  other arithmetic  49.8 us (7%)
  starting transfers between devices  30.8 us (4%)
  between operations  14.9 us (2%)
    psum x1, waiting for transfers between devices, per_device(): lax.psum((grad_attn_gain, grad_qkv, grad_attn_out, grad_mlp_gain, grad_ml...  268 us
    psum x1, blocking collectives, per_device(): lax.psum((grad_attn_gain, grad_qkv, grad_attn_out, grad_mlp_gain, grad_ml...  43.1 us
    unnamed x102, local copies, waits for them, and re-layouts  30.9 us
    all_to_all x1, blocking collectives, per_device(): lax.all_to_all(mixed_heads, 'seq', split_axis=1, concat_axis=2, tiled=True)  29.5 us
    all_to_all x1, waiting for transfers between devices, per_device(): lax.all_to_all(grad_head_v, 'seq', split_axis=1, concat_axis=2, tiled=True)  23.1 us
    all_to_all x1, waiting for transfers between devices, per_device(): lax.all_to_all(grad_head_q, 'seq', split_axis=1, concat_axis=2, tiled=True)  23.1 us
    all_to_all x1, waiting for transfers between devices, per_device(): lax.all_to_all(grad_attended, 'seq', split_axis=2, concat_axis=1, tiled=T...  17.4 us
    all_to_all x1, waiting for transfers between devices, per_device(): lax.all_to_all(queries, 'seq', split_axis=2, concat_axis=1, tiled=True)  16.6 us
  transfers between devices with their start and end apart: 8, of which 6 were waited for; matrix products, arithmetic and copies ran while one was open for 12% of the time, Pallas kernels for 0%

commit v1 on v0

--- a/solution.py
+++ b/solution.py
@@ -225,8 +225,11 @@
         (grad_input + grad_hidden).astype(jnp.bfloat16).reshape(doc_count, row_count, features)
     )
     summed = lax.psum(
-        (grad_attn_gain, grad_qkv, grad_attn_out, grad_mlp_gain, grad_mlp_in, grad_mlp_out),
-        ("doc", "seq"),
+        lax.psum(
+            (grad_attn_gain, grad_qkv, grad_attn_out, grad_mlp_gain, grad_mlp_in, grad_mlp_out),
+            "seq",
+        ),
+        "doc",
     )
     return (output, grad_input, summed[0], summed[1], summed[2], summed[3], summed[4], summed[5])
 

time: 752 us -> 1360 us (1.81)
  waiting for transfers between devices: 364 us -> 989 us
  blocking collectives: 72.7 us -> 53.3 us
    psum x1, waiting for transfers between devices: 268 us -> 672 us  [per_device(): lax.psum((grad_attn_gain, grad_qkv, grad_attn_out, grad_mlp_gain, grad_ml...]
    psum x0 -> x1, waiting for transfers between devices: none -> 222 us  [per_device(): lax.psum(lax.psum((grad_attn_gain, grad_qkv, grad_attn_out, grad_mlp_gain...]
    psum x1, blocking collectives: 43.1 us -> 9.53 us  [per_device(): lax.psum((grad_attn_gain, grad_qkv, grad_attn_out, grad_mlp_gain, grad_ml...]
    psum x0 -> x1, blocking collectives: none -> 14.3 us  [per_device(): lax.psum(lax.psum((grad_attn_gain, grad_qkv, grad_attn_out, grad_mlp_gain...]
  transfers between devices with their start and end apart: 8 -> 9, of which waited for: 6 -> 7; matrix products, arithmetic and copies ran while one was open for 12% -> 6% of each run, Pallas kernels for 0% -> 0%
where the time goes in v1:
time: 1360 us; the launch traced here: 1350 us
  waiting for transfers between devices  989 us (73%)
  local copies, waits for them, and re-layouts  133 us (10%)
  matrix products  77.8 us (6%)
  blocking collectives  53.3 us (4%)
  other arithmetic  49.9 us (4%)
  starting transfers between devices  30.8 us (2%)
  between operations  14.9 us (1%)
    psum x1, waiting for transfers between devices, per_device(): lax.psum((grad_attn_gain, grad_qkv, grad_attn_out, grad_mlp_gain, grad_ml...  672 us
    psum x1, waiting for transfers between devices, per_device(): lax.psum(lax.psum((grad_attn_gain, grad_qkv, grad_attn_out, grad_mlp_gain...  222 us
    unnamed x102, local copies, waits for them, and re-layouts  30.7 us
    all_to_all x1, blocking collectives, per_device(): lax.all_to_all(mixed_heads, 'seq', split_axis=1, concat_axis=2, tiled=True)  29.5 us
  transfers between devices with their start and end apart: 9, of which 7 were waited for; matrix products, arithmetic and copies ran while one was open for 6% of the time, Pallas kernels for 0%

profile of v1, /device:TPU:0, one launch (start us, length us, event | category | flops | bytes accessed | tf_op | source)
XLA Modules:
  0.0 1348.9 jit_solution(8615729528079659737)
XLA Ops:
  12.8 4.3 fusion.13
  23.3 6.3 all-to-all-start
  29.6 3.9 fusion.58
  59.2 5.0 add_convert_fusion.3
  67.2 5.1 all-to-all-start.1
  75.3 16.6 %all-to-all-done.1 = bf16[2,256,768]{1,0,2:T(2,128)(2,1)} async-done(((bf16[2,256,768]{1,0,2:T(2,128)(2,1)}), bf16[2,256,768]{1,0,2:T(2,128)(2,1)}, u32[]{:S(2)}, u32[]{:S(2)}) %all-to-all-start.1) | async-done | bytes 786464 | tf_op jit(solution)/shard_map/all_to_all | solution.py:148
  91.9 4.4 all-to-all-start.2
  100.7 15.2 %all-to-all-done.2 = bf16[2,256,768]{1,0,2:T(2,128)(2,1)} async-done(((bf16[2,256,768]{1,0,2:T(2,128)(2,1)}), bf16[2,256,768]{1,0,2:T(2,128)(2,1)}, u32[]{:S(2)}, u32[]{:S(2)}) %all-to-all-start.2) | async-done | bytes 786464 | tf_op jit(solution)/shard_map/all_to_all | solution.py:149
  119.2 19.5 %while.26 = (s32[]{:T(128)}, bf16[2,1024,192]{1,2,0:T(8,128)(2,1)}, f32[2,3,1024]{2,1,0:T(4,128)}, bf16[2,1024,192]{1,2,0:T(8,128)(2,1)}, bf16[2,1024,192]{1,2,0...) while((s32[]{:T(128)}, bf16[2,1024,192]{1,2,0:T(8,128)(2,1)}, f32[2,3,1024]{2,1,0:T(4,128)}, ...), condition=%wide.region_5.6_spmd, body=%wide.region_2.5_spmd.sunk | while | flops 833811456 | bytes 48861340 | solution.py:152
  142.3 29.5 %all_to_all.132 = bf16[2,1024,192]{2,0,1:T(2,128)(2,1)} all-to-all(bf16[2,1024,192]{2,0,1:T(2,128)(2,1)} %copy.86), channel_id=1, replica_groups=mesh['doc'=8,'seq'=4] {'seq'}, dimensions={1} | all-to-all | bytes 1572864 | tf_op jit(solution)/shard_map/all_to_all | solution.py:155
  171.8 5.9 copy.87
  184.3 5.6 fusion.39
  205.8 17.4 %all-to-all-done.4 = bf16[2,256,768]{1,0,2:T(2,128)(2,1)S(1)} async-done(((bf16[2,256,768]{1,0,2:T(2,128)(2,1)}), bf16[2,256,768]{1,0,2:T(2,128)(2,1)S(1)}, u32[]{:S(2)}, u32[]{:S(2)}) %all-to-all-start.4) | async-done | bytes 786464 | tf_op jit(solution)/shard_map/all_to_all | solution.py:188
  227.3 60.3 %while.27 = (s32[]{:T(128)}, bf16[2,1024,192]{1,2,0:T(8,128)(2,1)}, bf16[2,1024,192]{1,2,0:T(8,128)(2,1)}, bf16[2,1024,192]{1,2,0:T(8,128)(2,1)}, bf16[2,1024,19...) while((s32[]{:T(128)}, bf16[2,1024,192]{1,2,0:T(8,128)(2,1)}, ...), condition=%wide.region_12.13_spmd, body=%wide.region_10.12_spmd.sunk | while | flops 2053501952 | bytes 154489168 | solution.py:190
  242.4 5.3 multiply_convert_fusion.6
  247.7 4.1 convolution_bitcast_fusion.3
  272.6 5.3 multiply_convert_fusion.6
  277.9 4.1 convolution_bitcast_fusion.3
  296.8 23.1 %all-to-all-done.7 = bf16[2,1024,192]{2,0,1:T(2,128)(2,1)S(1)} async-done(((bf16[2,1024,192]{2,0,1:T(2,128)(2,1)}), bf16[2,1024,192]{2,0,1:T(2,128)(2,1)S(1)}, u32[]{:S(2)}, u32[]{:S(2)}) %all-to-all-start.7) | async-done | bytes 786464 | tf_op jit(solution)/shard_map/all_to_all | solution.py:197
  325.6 23.1 %all-to-all-done.5 = bf16[2,1024,192]{2,0,1:T(2,128)(2,1)S(1)} async-done(((bf16[2,1024,192]{2,0,1:T(2,128)(2,1)}), bf16[2,1024,192]{2,0,1:T(2,128)(2,1)S(1)}, u32[]{:S(2)}, u32[]{:S(2)}) %all-to-all-start.5) | async-done | bytes 786464 | tf_op jit(solution)/shard_map/all_to_all | solution.py:195
  348.7 4.2 all-to-all-start.6
  361.0 5.2 fusion.40
  366.2 4.7 copy.96
  372.0 5.7 copy.92
  379.9 5.7 copy.94
  394.3 672.0 %all-reduce.11.cloned.1.call-done = (f32[768,2304]{0,1:T(8,128)}, f32[768,768]{1,0:T(8,128)}, f32[768,2304]{1,0:T(8,128)}, f32[1152,768]{1,0:T(8,128)}) async-done(((f32[768,2304]{0,1:T(8,128)}, f32[768,768]{1,0:T(8,128)}, f32[768,2304]{1,0:T(8,128)}, f32[1152,768]{1,0:T(8,128)}), (f32[768,2304]{0,1:T(8,128)}, f32[768,768]{1,0:T(8,128)}, f32[768,2304]{1,0:T(8,128)}, ...) | async-done | bytes 20054032 | tf_op jit(solution)/shard_map/psum | solution.py:228
  1067.0 4.1 add_convert_fusion.2
  1075.6 9.5 all-reduce.4
  1085.1 14.3 %all-reduce.2 = (f32[768]{0:T(1024)}, f32[768]{0:T(1024)}) all-reduce(f32[768]{0:T(1024)S(1)} %get-tuple-element.181, f32[768]{0:T(1024)S(1)} %get-tuple-element.182), channel_id=1, replica_groups=mesh['doc'=8,'seq'=4] {'doc'}, use_global_device_ids=true, to_apply=%region_17.18 | all-reduce | flops 1536 | bytes 12288 | tf_op jit(solution)/shard_map/psum | solution.py:227
  1102.4 221.5 %all-reduce.9.cloned.1.call-done = (f32[768,2304]{0,1:T(8,128)}, f32[768,768]{1,0:T(8,128)}, f32[768,2304]{1,0:T(8,128)}, f32[1152,768]{1,0:T(8,128)}) async-done(((f32[768,2304]{0,1:T(8,128)}, f32[768,768]{1,0:T(8,128)}, f32[768,2304]{1,0:T(8,128)}, f32[1152,768]{1,0:T(8,128)}), (f32[768,2304]{0,1:T(8,128)}, f32[768,768]{1,0:T(8,128)}, f32[768,2304]{1,0:T(8,128)}, ...) | async-done | bytes 20054032 | tf_op jit(solution)/shard_map/psum | solution.py:227
  1324.0 8.1 copy.97
  1333.5 6.6 copy.149
  (256 shorter events, 188.0 us)
Async XLA Ops:
  7.2 174.9 %copy-start = (bf16[768,2304]{1,0:T(8,128)(2,1)S(1)}, bf16[768,2304]{1,0:T(8,128)(2,1)}, u32[]{:S(2)}) copy-start(bf16[768,2304]{1,0:T(8,128)(2,1)} %param.17) | copy-start | bytes 10616836
  12.8 4.3 copy-start.8
  23.3 43.9 %all-to-all-start = ((bf16[2,256,768]{1,0,2:T(2,128)(2,1)}), bf16[2,256,768]{1,0,2:T(2,128)(2,1)}, u32[]{:S(2)}, u32[]{:S(2)}) async-start(bf16[2,256,768]{1,0,2:T(2,128)(2,1)} %copy.71), calls=%async_computation | async-start | bytes 1572864 | tf_op jit(solution)/shard_map/all_to_all | solution.py:150
  33.4 8.8 copy-start.50
  67.2 24.7 %all-to-all-start.1 = ((bf16[2,256,768]{1,0,2:T(2,128)(2,1)}), bf16[2,256,768]{1,0,2:T(2,128)(2,1)}, u32[]{:S(2)}, u32[]{:S(2)}) async-start(bf16[2,256,768]{1,0,2:T(2,128)(2,1)} %copy.78), calls=%async_computation.1 | async-start | bytes 1572864 | tf_op jit(solution)/shard_map/all_to_all | solution.py:148
  91.9 24.0 %all-to-all-start.2 = ((bf16[2,256,768]{1,0,2:T(2,128)(2,1)}), bf16[2,256,768]{1,0,2:T(2,128)(2,1)}, u32[]{:S(2)}, u32[]{:S(2)}) async-start(bf16[2,256,768]{1,0,2:T(2,128)(2,1)} %copy.83), calls=%async_computation.2 | async-start | bytes 1572864 | tf_op jit(solution)/shard_map/all_to_all | solution.py:149
  181.7 13.2 copy-start.6
  181.8 13.2 copy-start.41
  182.1 12.9 copy-start.43
  198.8 5.3 copy-start.51
  200.6 22.6 %all-to-all-start.4 = ((bf16[2,256,768]{1,0,2:T(2,128)(2,1)}), bf16[2,256,768]{1,0,2:T(2,128)(2,1)S(1)}, u32[]{:S(2)}, u32[]{:S(2)}) async-start(bf16[2,256,768]{1,0,2:T(2,128)(2,1)} %copy.88), calls=%async_computation.4 | async-start | bytes 1572864 | tf_op jit(solution)/shard_map/all_to_all | solution.py:188
  247.7 4.6 copy-start.2
  277.9 4.6 copy-start.2
  287.6 7.2 copy-start.22
  291.3 28.7 %all-to-all-start.7 = ((bf16[2,1024,192]{2,0,1:T(2,128)(2,1)}), bf16[2,1024,192]{2,0,1:T(2,128)(2,1)S(1)}, u32[]{:S(2)}, u32[]{:S(2)}) async-start(bf16[2,1024,192]{2,0,1:T(2,128)(2,1)} %copy.95), calls=%async_computation.7 | async-start | bytes 2097152 | tf_op jit(solution)/shard_map/all_to_all | solution.py:197
  294.8 28.7 %copy-start.25 = (bf16[2,1024,192]{1,2,0:T(8,128)(2,1)S(1)}, bf16[2,1024,192]{1,2,0:T(8,128)(2,1)}, u32[]{:S(2)}) copy-start(bf16[2,1024,192]{1,2,0:T(8,128)(2,1)} %get-tuple-element.103) | copy-start | bytes 2359300
  320.0 28.7 %copy-start.17 = (bf16[2,1024,192]{2,0,1:T(2,128)(2,1)}, bf16[2,1024,192]{2,0,1:T(2,128)(2,1)S(1)}, u32[]{:S(2)}) copy-start(bf16[2,1024,192]{2,0,1:T(2,128)(2,1)S(1)} %all-to-all-done.7) | copy-start | bytes 2359300
  320.0 28.7 %all-to-all-start.5 = ((bf16[2,1024,192]{2,0,1:T(2,128)(2,1)}), bf16[2,1024,192]{2,0,1:T(2,128)(2,1)S(1)}, u32[]{:S(2)}, u32[]{:S(2)}) async-start(bf16[2,1024,192]{2,0,1:T(2,128)(2,1)} %copy.91), calls=%async_computation.5 | async-start | bytes 2097152 | tf_op jit(solution)/shard_map/all_to_all | solution.py:195
  348.7 8.1 copy-start.18
  348.7 31.2 %all-to-all-start.6 = ((bf16[2,1024,192]{2,0,1:T(2,128)(2,1)}), bf16[2,1024,192]{2,0,1:T(2,128)(2,1)}, u32[]{:S(2)}, u32[]{:S(2)}) async-start(bf16[2,1024,192]{2,0,1:T(2,128)(2,1)} %copy.93), calls=%async_computation.6 | async-start | bytes 2097152 | tf_op jit(solution)/shard_map/all_to_all | solution.py:196
  353.0 713.4 %all-reduce.11.cloned.1.call-start = ((), (), s32[]{:S(2)}) async-start(), calls=%async_computation.9 | async-start | bytes 40108032 | tf_op jit(solution)/shard_map/psum | solution.py:228
  356.9 4.1 copy-start.36
  356.9 4.1 copy-start.39
  356.9 4.1 copy-start.42
  356.9 4.1 copy-start.44
  377.7 9.3 copy-start.9
  394.3 929.7 %all-reduce.9.cloned.1.call-start = ((), (), s32[]{:S(2)}) async-start(), calls=%async_computation.8 | async-start | bytes 40108032 | tf_op jit(solution)/shard_map/psum | solution.py:227
  1067.0 4.1 copy-start.30
  1074.8 24.6 %copy-start.46 = (f32[512]{0:T(512)S(1)}, f32[512]{0:T(512)}, u32[]{:S(2)}) copy-start(f32[512]{0:T(512)} %copy-done.45) | copy-start | bytes 6148
  1324.0 8.1 copy-start.34
  1333.5 6.6 copy-start.19
  1333.5 8.4 copy-start.1
  (39 other events, 71.7 us)
Sparse Core Ops, SparseCore 0:
  394.4 671.8 all-reduce.10
  1070.6 253.2 all-reduce.8
